TPU v7x, 32 devices: a whole 2x2x4 slice. The times are simulated.
32 devices in a mesh: img: 8 (over z, y), pix: 4 (over x, core).
Axes of the slice: x: 2, y: 2, z: 4, core: 2. Of those that a mesh axis runs over, the one named last changes fastest.
Arguments:
- images: bfloat16 [3072, 16384], P('img', 'pix'), may hold values from -12 to 12
- inverse_noise_scale: float32 [3072], P('img'), may hold values from 0.4 to 4
- projections: bfloat16 [8192, 16384], P('img', 'pix'), may hold values from -1 to 1
- group_search_blocks: int32 [8, 16], P('img'), may hold values from 0 to 63, as said below
- search_list_count: int32 [8], P('img'), may hold values from 12 to 16, as said below
Outputs:
- projection_sums: float32 [8192, 16384], P('img', 'pix')
- log_evidence: float32 [3072], P(('img', 'pix'))
Inputs may be any that keep to these rules, and one draw needn't show every extreme that they name: `group_search_blocks`: each row lists 16 different block ids; block b is owned by index b // 8 of img. Among the first search_list_count[g] entries of row g no owner appears more than 2 times, and in every draw one owner has 2 of its blocks among the first 2 entries of every row. `search_list_count`: some group's count is 16 in every draw.
All inputs are finite; a program needn't handle non-finite values.
Results may differ from a plain program's by a relative error of at most 0.004.
Values may be sent and summed in bfloat16 or wider, within the bound.
No kernel may reach another device: no remote copies, remote signals or barrier semaphores. Data moves between devices by JAX's collectives and lax.ppermute only.
A program may use at most 128 MiB of HBM per device.

v0:
```python
import jax
import jax.numpy as jnp
from jax import lax
from jax.sharding import PartitionSpec as P

BLOCK = 128
CAP = 2
MAXL = 16


def normalise(totals, scaling, slot_used):
    logits = totals * scaling[None, :, None, None]
    live_mask = slot_used[:, None, :, None]
    logits = jnp.where(live_mask, logits, jnp.float32(-1e30))
    row_peak = jnp.max(logits, axis=(0, 2, 3), keepdims=True)
    exponent = jnp.where(live_mask, jnp.exp(logits - row_peak), jnp.float32(0.0))
    row_total = jnp.sum(exponent, axis=(0, 2, 3), keepdims=True)
    weights = (exponent / row_total).astype(jnp.bfloat16)
    marginal_likelihood = (row_peak + jnp.log(row_total)).reshape(-1)
    return (weights, marginal_likelihood)


def on_device(images, inverse_noise_scale, projections, group_search_blocks, search_list_count):
    group_rows, pixels = images.shape
    n_groups = lax.axis_size("img")
    n_shares = lax.axis_size("pix")
    owned_blocks = projections.shape[0] // BLOCK
    every_list, every_count = (
        lax.all_gather(group_search_blocks, "img", axis=0, tiled=True),
        lax.all_gather(search_list_count, "img", axis=0, tiled=True),
    )
    own_index = lax.axis_index("img")
    positions = jnp.arange(MAXL, dtype=jnp.int32)
    slot_ids = jnp.arange(CAP, dtype=jnp.int32)
    live_entry = positions[None, :] < every_count[:, None]
    local_hit = live_entry & (every_list // owned_blocks == own_index)
    slot_rank = jnp.cumsum(local_hit.astype(jnp.int32), axis=1) - 1
    slot_pick = local_hit[:, None, :] & (slot_rank[:, None, :] == slot_ids[None, :, None])
    slot_offset = jnp.sum(jnp.where(slot_pick, every_list[:, None, :] % owned_blocks, 0), axis=2)
    slot_filled = jnp.any(slot_pick, axis=2)
    own_live = positions < search_list_count[0]
    own_owner = group_search_blocks[0] // owned_blocks
    per_owner = jnp.sum(
        (
            own_live[None, :]
            & (own_owner[None, :] == jnp.arange(n_groups, dtype=jnp.int32)[:, None])
        ).astype(jnp.int32),
        axis=1,
    )
    slot_used = slot_ids[None, :] < per_owner[:, None]
    stacked = projections.reshape(owned_blocks, BLOCK, pixels)
    outgoing = jnp.take(stacked, slot_offset.reshape(-1), axis=0).reshape(
        n_groups, CAP, BLOCK, pixels
    )
    everyone = lax.all_gather(images, "img", axis=0, tiled=True).reshape(
        n_groups, group_rows, pixels
    )
    local_scores = jnp.einsum(
        "gcrf,gif->gicr", outgoing, everyone, preferred_element_type=jnp.float32
    )
    partial_value = lax.all_to_all(local_scores, "img", split_axis=0, concat_axis=0, tiled=True)
    share_rows = group_rows // n_shares
    first_row = lax.axis_index("pix") * share_rows
    totals = lax.psum(partial_value, "pix")
    weights, marginal_likelihood = normalise(totals, inverse_noise_scale, slot_used)
    evidence_out = lax.dynamic_slice_in_dim(marginal_likelihood, first_row, share_rows)
    weights_home = lax.all_to_all(weights, "img", split_axis=0, concat_axis=0, tiled=True)
    arriving = jnp.einsum(
        "gicr,gif->gcrf", weights_home, everyone, preferred_element_type=jnp.float32
    ).astype(jnp.bfloat16)
    placement = (
        slot_offset.reshape(-1)[None, :] == jnp.arange(owned_blocks, dtype=jnp.int32)[:, None]
    ) & slot_filled.reshape(-1)[None, :]
    placement_table = placement.astype(jnp.bfloat16)
    running_total = jnp.dot(
        placement_table,
        arriving.reshape(n_groups * CAP, BLOCK * pixels),
        preferred_element_type=jnp.float32,
    )
    return (running_total.reshape(owned_blocks * BLOCK, pixels), evidence_out)


def solution(mesh):
    placed = (P("img", "pix"), P("img"), P("img", "pix"), P("img", None), P("img"))
    return jax.shard_map(
        on_device,
        mesh=mesh,
        in_specs=placed,
        out_specs=(P("img", "pix"), P(("img", "pix"))),
        check_vma=False,
    )
```

profile of v0, /device:TPU:0, one launch (start us, length us, event | category | flops | bytes accessed | tf_op | source)
XLA Modules:
  0.0 769.8 jit_solution(3247662707351451047)
XLA Ops:
  7.2 0.0 copy-start.3
  7.2 0.0 copy-start.2
  7.2 0.0 all-gather.3.cloned.1.call-start
  7.2 0.7 all-gather.3.cloned.1.call-update
  7.9 0.0 all-reduce.3.cloned.1.call-start
  8.6 0.0 copy-done.3
  8.6 0.6 dynamic-slice.2
  9.2 0.8 dynamic-update-slice
  10.0 13.3 %all-reduce = s32[8]{0:T(128)S(1)} all-reduce(s32[8]{0:T(128)S(1)} %dynamic-update-slice), channel_id=1, replica_groups=mesh['img'=8,'pix'=4] {'img'}, use_global_device_ids=true, to_apply=%add | all-reduce | flops 8 | bytes 64
  23.3 0.0 copy-done.2
  23.3 43.3 %all-gather = s32[8,1,16]{2,1,0:T(1,128)S(1)} all-gather(s32[1,1,16]{2,1,0:T(1,128)S(1)} %bitcast.33), channel_id=1, replica_groups=mesh['img'=8,'pix'=4] {'img'}, dimensions={0}, use_global_device_ids=true | all-gather | bytes 576 | tf_op jit(solution)/shard_map/all_gather | solution.py:29
  66.6 0.1 fusion.24
  66.6 0.2 reduce_window_sum.11
  66.8 0.1 select_reduce_fusion
  67.0 0.1 copy.7
  67.1 0.1 copy.9
  67.2 0.1 reshape.124
  67.3 10.7 %gather_fusion = bf16[16,128,4096]{2,1,0:T(8,128)(2,1)} fusion(bf16[8,128,4096]{2,1,0:T(8,128)(2,1)} %bitcast.27, s32[1024]{0:T(1024)S(1)} %pad_clamp_fusion), kind=kCustom, calls=%fused_computation | custom fusion | bytes 33554496 | tf_op jit(solution)/shard_map/jit(_take)/gather | solution.py:52
  78.0 414.8 %all-gather.3.cloned.1.call-done = bf16[3072,4096]{1,0:T(8,128)(2,1)} async-done(((bf16[384,4096]{1,0:T(8,128)(2,1)}), bf16[3072,4096]{1,0:T(8,128)(2,1)}) %all-gather.3.cloned.1.call-update) | async-done | bytes 25165840 | tf_op jit(solution)/shard_map/all_gather | solution.py:55
  492.7 21.4 %fusion.6 = f32[8,384,2,128]{1,3,2,0:T(8,128)S(1)} fusion(bf16[8,384,4096,1]{2,1,3,0:T(8,128)(2,1)} %bitcast.28, bf16[8,2,128,4096]{3,2,1,0:T(8,128)(2,1)} %bitcast.30, pred[8,2]{1,0:T(8,128)(4,1)S(1)} %copy.9), kind=kOutput, calls=%fused_computation.11 | convolution fusion | flops 6450839552 | bytes 45088784 | tf_op jit(solution)/shard_map/gcrf,gif->gicr/dot_general | solution.py:58
  514.2 75.3 %all_to_all.10 = f32[8,384,2,128]{1,3,2,0:T(8,128)} all-to-all(f32[8,384,2,128]{1,3,2,0:T(8,128)S(1)} %fusion.6), channel_id=1, replica_groups=mesh['img'=8,'pix'=4] {'img'}, dimensions={0} | all-to-all | bytes 6291456 | tf_op jit(solution)/shard_map/all_to_all | solution.py:61
  589.5 0.0 copy-start.1
  589.5 0.0 all-reduce.3.cloned.1.call-update
  589.6 0.1 convert_reduce_fusion
  589.7 0.1 iota_compare_fusion.2
  589.8 67.4 %all-reduce.3.cloned.1.call-done = f32[8,384,2,128]{1,3,2,0:T(8,128)} async-done(((f32[8,384,2,128]{1,3,2,0:T(8,128)}), f32[8,384,2,128]{1,3,2,0:T(8,128)}) %all-reduce.3.cloned.1.call-update) | async-done | bytes 3145744 | tf_op jit(solution)/shard_map/psum | solution.py:64
  657.1 0.0 copy-done.1
  657.1 0.0 copy-start
  657.1 2.5 fusion.4
  659.7 0.3 copy-done
  660.0 0.8 fusion.5
  660.8 2.0 divide_convert_fusion
  662.8 5.5 all-to-all-start.1
  668.3 0.1 eq.56
  668.4 0.1 fusion.10
  668.6 0.1 copy.8
  668.7 0.1 and.62
  668.8 0.6 dynamic_slice.3
  669.4 35.7 %all-to-all-done.1 = bf16[8,384,2,128]{1,3,2,0:T(8,128)(2,1)S(1)} async-done(((bf16[8,384,2,128]{1,3,2,0:T(8,128)(2,1)}), bf16[8,384,2,128]{1,3,2,0:T(8,128)(2,1)S(1)}, u32[]{:S(2)}, u32[]{:S(2)}) %all-to-all-start.1) | async-done | bytes 1572896 | tf_op jit(solution)/shard_map/all_to_all | solution.py:67
  705.1 21.3 %convolution_convert_fusion = bf16[8,2,128,4096]{3,2,1,0:T(8,128)(2,1)} fusion(bf16[8,384,2,128]{1,3,2,0:T(8,128)(2,1)S(1)} %all-to-all-done.1, bf16[8,384,4096,1]{2,1,3,0:T(8,128)(2,1)} %bitcast.29), kind=kOutput, calls=%fused_computation.4 | convolution fusion | flops 6450839552 | bytes 43515904 | tf_op jit(solution)/shard_map/gicr,gif->gcrf/dot_general | solution.py:68
  726.3 14.8 %copy.12 = bf16[2,8,128,4096]{3,1,2,0:T(8,128)(2,1)S(1)} copy(bf16[2,8,128,4096]{3,2,1,0:T(8,128)(2,1)} %bitcast.26) | data formatting | bytes 33554432
  741.1 7.0 fusion.15
  748.1 14.9 %reshape.127 = f32[1024,4096]{1,0:T(8,128)} reshape(f32[8,524288]{1,0:T(8,128)} %fusion.15) | data formatting | bytes 33554432 | tf_op jit(solution)/shard_map/reshape | solution.py:80
  (9 shorter events, 0.1 us)
Async XLA Ops:
  7.2 1.5 copy-start.3
  7.2 16.1 %copy-start.2 = (s32[1,16]{1,0:T(1,128)S(1)}, s32[1,16]{1,0:T(1,128)}, u32[]{:S(2)}) copy-start(s32[1,16]{1,0:T(1,128)} %param.8) | copy-start | bytes 196
  7.2 485.5 %all-gather.3.cloned.1.call-start = ((), (), s32[]{:S(2)}) async-start(), calls=%async_computation.2 | async-start | bytes 28311552 | tf_op jit(solution)/shard_map/all_gather | solution.py:55
  7.9 649.2 %all-reduce.3.cloned.1.call-start = ((), (), s32[]{:S(2)}) async-start(), calls=%async_computation.3 | async-start | bytes 6291456 | tf_op jit(solution)/shard_map/psum | solution.py:64
  589.5 67.6 %copy-start.1 = (f32[384]{0:T(512)S(1)}, f32[384]{0:T(512)}, u32[]{:S(2)}) copy-start(f32[384]{0:T(512)} %param.6) | copy-start | bytes 4612
  657.1 2.8 copy-start
  662.8 42.2 %all-to-all-start.1 = ((bf16[8,384,2,128]{1,3,2,0:T(8,128)(2,1)}), bf16[8,384,2,128]{1,3,2,0:T(8,128)(2,1)S(1)}, u32[]{:S(2)}, u32[]{:S(2)}) async-start(bf16[8,384,2,128]{1,3,2,0:T(8,128)(2,1)} %divide_convert_fusion), calls=%async_computation.1 | async-start | bytes 3145728 | tf_op jit(solution)/shard_map/all_to_all | solution.py:67
Sparse Core Ops, SparseCore 0:
  9.5 483.1 all-gather.2
  589.7 67.4 all-reduce.2
where the time goes:
time: 770 us
  waiting for transfers between devices  519 us (67%)
  blocking collectives  132 us (17%)
  matrix products  49.7 us (6%)
  local copies, waits for them, and re-layouts  43.1 us (6%)
  between operations  14.8 us (2%)
    all_gather x1, waiting for transfers between devices, on_device(): lax.all_gather(images, 'img', axis=0, tiled=True)  415 us
    all_to_all x1, blocking collectives, on_device(): lax.all_to_all(local_scores, 'img', split_axis=0, concat_axis=0, tiled=True)  75.3 us
    psum x1, waiting for transfers between devices, on_device(): totals = lax.psum(partial_value, 'pix')  67.4 us
    all_gather x1, blocking collectives, on_device(): lax.all_gather(group_search_blocks, 'img', axis=0, tiled=True)  43.3 us
    all_to_all x1, waiting for transfers between devices, on_device(): lax.all_to_all(weights, 'img', split_axis=0, concat_axis=0, tiled=True)  35.7 us
    dot_general x1, matrix products, on_device(): jnp.einsum('gcrf,gif->gicr', outgoing, everyone, preferred_element_type=j...  21.4 us
    dot_general x1, matrix products, on_device(): jnp.einsum('gicr,gif->gcrf', weights_home, everyone, preferred_element_ty...  21.3 us
    unnamed x12, local copies, waits for them, and re-layouts  16.4 us
  transfers between devices with their start and end apart: 3, of which 3 were waited for; matrix products, arithmetic and copies ran while one was open for 2% of the time, Pallas kernels for 0%

commit v1 on v0

--- a/solution.py
+++ b/solution.py
@@ -1,11 +1,21 @@
+import functools
 import jax
 import jax.numpy as jnp
 from jax import lax
 from jax.sharding import PartitionSpec as P
+from jax.lax import all_gather
 
 BLOCK = 128
 CAP = 2
 MAXL = 16
+
+
+def time_zones_by_axis(values, axis_name):
+    local_out = all_gather(values, axis_name=axis_name)
+    return jnp.sum(local_out, axis=0)
+
+
+reach_the_group = functools.partial(time_zones_by_axis, axis_name="pix")
 
 
 def normalise(totals, scaling, slot_used):
@@ -61,7 +71,7 @@
     partial_value = lax.all_to_all(local_scores, "img", split_axis=0, concat_axis=0, tiled=True)
     share_rows = group_rows // n_shares
     first_row = lax.axis_index("pix") * share_rows
-    totals = lax.psum(partial_value, "pix")
+    totals = reach_the_group(partial_value)
     weights, marginal_likelihood = normalise(totals, inverse_noise_scale, slot_used)
     evidence_out = lax.dynamic_slice_in_dim(marginal_likelihood, first_row, share_rows)
     weights_home = lax.all_to_all(weights, "img", split_axis=0, concat_axis=0, tiled=True)

time: 770 us -> 792 us (1.029)
  waiting for transfers between devices: 519 us -> 533 us
    all_gather x0 -> x1, waiting for transfers between devices: none -> 81 us  [time_zones_by_axis(): local_out = all_gather(values, axis_name=axis_name)]
    psum x1 -> x0, waiting for transfers between devices: 67.4 us -> none  [on_device(): totals = lax.psum(partial_value, 'pix')]
    unnamed x12 -> x10, local copies, waits for them, and re-layouts: 16.4 us -> 16.1 us
where the time goes in v1:
time: 792 us; the launch traced here: 791 us
  waiting for transfers between devices  533 us (67%)
  blocking collectives  132 us (17%)
  local copies, waits for them, and re-layouts  47.6 us (6%)
  matrix products  46.9 us (6%)
  between operations  14.8 us (2%)
  other arithmetic  11.6 us (1%)
    all_gather x1, waiting for transfers between devices, on_device(): lax.all_gather(images, 'img', axis=0, tiled=True)  415 us
    all_gather x1, waiting for transfers between devices, time_zones_by_axis(): local_out = all_gather(values, axis_name=axis_name)  81 us
    all_to_all x1, blocking collectives, on_device(): lax.all_to_all(local_scores, 'img', split_axis=0, concat_axis=0, tiled=True)  75.4 us
    all_gather x1, blocking collectives, on_device(): lax.all_gather(group_search_blocks, 'img', axis=0, tiled=True)  43.3 us
    all_to_all x1, waiting for transfers between devices, on_device(): lax.all_to_all(weights, 'img', split_axis=0, concat_axis=0, tiled=True)  36.4 us
    dot_general x1, matrix products, on_device(): jnp.einsum('gicr,gif->gcrf', weights_home, everyone, preferred_element_ty...  21.3 us
    dot_general x1, matrix products, on_device(): jnp.einsum('gcrf,gif->gicr', outgoing, everyone, preferred_element_type=j...  18.7 us
    unnamed x10, local copies, waits for them, and re-layouts  16.1 us
  transfers between devices with their start and end apart: 3, of which 3 were waited for; matrix products, arithmetic and copies ran while one was open for 2% of the time, Pallas kernels for 0%

profile of v1, /device:TPU:0, one launch (start us, length us, event | category | flops | bytes accessed | tf_op | source)
XLA Modules:
  0.0 791.4 jit_solution(3262616589814463363)
XLA Ops:
  7.2 0.0 copy-start.2
  7.2 0.0 copy-start.1
  7.2 0.0 all-gather.5.cloned.1.call-start
  7.2 0.7 all-gather.5.cloned.1.call-update
  7.9 0.0 all-gather.7.cloned.1.call-start
  8.6 0.0 copy-done.2
  8.6 0.6 dynamic-slice.2
  9.2 0.8 dynamic-update-slice
  10.0 13.3 %all-reduce = s32[8]{0:T(128)S(1)} all-reduce(s32[8]{0:T(128)S(1)} %dynamic-update-slice), channel_id=1, replica_groups=mesh['img'=8,'pix'=4] {'img'}, use_global_device_ids=true, to_apply=%add | all-reduce | flops 8 | bytes 64
  23.3 0.0 copy-done.1
  23.3 43.3 %all-gather.1 = s32[8,1,16]{2,1,0:T(1,128)S(1)} all-gather(s32[1,1,16]{2,1,0:T(1,128)S(1)} %bitcast.35), channel_id=1, replica_groups=mesh['img'=8,'pix'=4] {'img'}, dimensions={0}, use_global_device_ids=true | all-gather | bytes 576 | tf_op jit(solution)/shard_map/all_gather | solution.py:39
  66.6 0.1 fusion.24
  66.6 0.2 reduce_window_sum.11
  66.8 0.1 select_reduce_fusion
  67.0 0.1 copy.10
  67.1 0.1 copy.12
  67.2 0.1 reshape.124
  67.3 10.7 %gather_fusion = bf16[16,128,4096]{2,1,0:T(8,128)(2,1)} fusion(bf16[8,128,4096]{2,1,0:T(8,128)(2,1)} %bitcast.28, s32[1024]{0:T(1024)S(1)} %pad_clamp_fusion), kind=kCustom, calls=%fused_computation | custom fusion | bytes 33554496 | tf_op jit(solution)/shard_map/jit(_take)/gather | solution.py:62
  78.0 414.8 %all-gather.5.cloned.1.call-done = bf16[3072,4096]{1,0:T(8,128)(2,1)} async-done(((bf16[384,4096]{1,0:T(8,128)(2,1)}), bf16[3072,4096]{1,0:T(8,128)(2,1)}) %all-gather.5.cloned.1.call-update) | async-done | bytes 25165840 | tf_op jit(solution)/shard_map/all_gather | solution.py:65
  492.7 18.7 %fusion.6 = f32[8,384,2,128]{1,3,2,0:T(8,128)} fusion(bf16[8,384,4096,1]{2,1,3,0:T(8,128)(2,1)} %bitcast.29, bf16[8,2,128,4096]{3,2,1,0:T(8,128)(2,1)} %bitcast.31, pred[8,2]{1,0:T(8,128)(4,1)S(1)} %copy.12), kind=kOutput, calls=%fused_computation.11 | convolution fusion | flops 6450839552 | bytes 45088784 | tf_op jit(solution)/shard_map/gcrf,gif->gicr/dot_general | solution.py:68
  511.4 75.4 %all_to_all.10 = f32[8,384,2,128]{1,3,2,0:T(8,128)S(1)} all-to-all(f32[8,384,2,128]{1,3,2,0:T(8,128)} %fusion.6), channel_id=1, replica_groups=mesh['img'=8,'pix'=4] {'img'}, dimensions={0} | all-to-all | bytes 6291456 | tf_op jit(solution)/shard_map/all_to_all | solution.py:71
  586.8 2.4 copy.14
  589.2 0.0 all-gather.7.cloned.1.call-update
  589.2 0.1 convert_reduce_fusion
  589.4 0.1 iota_compare_fusion.2
  589.4 81.0 %all-gather.7.cloned.1.call-done = f32[32,384,2,128]{3,1,2,0:T(8,128)} async-done(((f32[8,384,2,128]{3,1,2,0:T(8,128)}), f32[32,384,2,128]{3,1,2,0:T(8,128)}) %all-gather.7.cloned.1.call-update) | async-done | bytes 12582928 | tf_op jit(solution)/shard_map/all_gather | solution.py:14
  670.5 7.5 reduce_sum.38
  678.0 0.0 copy-start
  678.0 2.4 copy.15
  680.4 0.0 copy-done
  680.4 0.5 fusion.4
  680.9 0.8 fusion.5
  681.7 2.0 divide_convert_fusion
  683.7 5.5 all-to-all-start.1
  689.2 0.1 eq.56
  689.3 0.1 fusion.10
  689.4 0.1 copy.11
  689.5 0.1 and.62
  689.6 0.6 dynamic_slice.3
  690.2 36.4 %all-to-all-done.1 = bf16[8,384,2,128]{1,3,2,0:T(8,128)(2,1)S(1)} async-done(((bf16[8,384,2,128]{1,3,2,0:T(8,128)(2,1)}), bf16[8,384,2,128]{1,3,2,0:T(8,128)(2,1)S(1)}, u32[]{:S(2)}, u32[]{:S(2)}) %all-to-all-start.1) | async-done | bytes 1572896 | tf_op jit(solution)/shard_map/all_to_all | solution.py:77
  726.6 21.3 %convolution_convert_fusion = bf16[8,2,128,4096]{3,2,1,0:T(8,128)(2,1)} fusion(bf16[8,384,2,128]{1,3,2,0:T(8,128)(2,1)S(1)} %all-to-all-done.1, bf16[8,384,4096,1]{2,1,3,0:T(8,128)(2,1)} %bitcast.30), kind=kOutput, calls=%fused_computation.4 | convolution fusion | flops 6450839552 | bytes 43515904 | tf_op jit(solution)/shard_map/gicr,gif->gcrf/dot_general | solution.py:78
  747.9 14.8 %copy.17 = bf16[2,8,128,4096]{3,1,2,0:T(8,128)(2,1)S(1)} copy(bf16[2,8,128,4096]{3,2,1,0:T(8,128)(2,1)} %bitcast.27) | data formatting | bytes 33554432
  762.7 7.0 fusion.15
  769.6 14.9 %reshape.127 = f32[1024,4096]{1,0:T(8,128)} reshape(f32[8,524288]{1,0:T(8,128)} %fusion.15) | data formatting | bytes 33554432 | tf_op jit(solution)/shard_map/reshape | solution.py:90
  (9 shorter events, 0.1 us)
Async XLA Ops:
  7.2 1.5 copy-start.2
  7.2 16.1 %copy-start.1 = (s32[1,16]{1,0:T(1,128)S(1)}, s32[1,16]{1,0:T(1,128)}, u32[]{:S(2)}) copy-start(s32[1,16]{1,0:T(1,128)} %param.8) | copy-start | bytes 196
  7.2 485.5 %all-gather.5.cloned.1.call-start = ((), (), s32[]{:S(2)}) async-start(), calls=%async_computation.2 | async-start | bytes 28311552 | tf_op jit(solution)/shard_map/all_gather | solution.py:65
  7.9 662.5 %all-gather.7.cloned.1.call-start = ((), (), s32[]{:S(2)}) async-start(), calls=%async_computation.3 | async-start | bytes 15728640 | tf_op jit(solution)/shard_map/all_gather | solution.py:14
  678.0 2.4 copy-start
  683.7 42.9 %all-to-all-start.1 = ((bf16[8,384,2,128]{1,3,2,0:T(8,128)(2,1)}), bf16[8,384,2,128]{1,3,2,0:T(8,128)(2,1)S(1)}, u32[]{:S(2)}, u32[]{:S(2)}) async-start(bf16[8,384,2,128]{1,3,2,0:T(8,128)(2,1)} %divide_convert_fusion), calls=%async_computation.1 | async-start | bytes 3145728 | tf_op jit(solution)/shard_map/all_to_all | solution.py:77
Sparse Core Ops, SparseCore 0:
  9.5 483.1 all-gather.4
  589.3 81.0 all-gather.6
